TPU v7x, 32 devices: a whole 2x2x4 slice. The times are simulated.
32 devices in a mesh: replica: 8 (over z, y), tp: 4 (over x, core).
Axes of the slice: x: 2, y: 2, z: 4, core: 2. Of those that a mesh axis runs over, the one named last changes fastest.
Arguments:
- hidden: bfloat16 [96, 4, 8192], P('replica', None, 'tp'), may hold values from -6 to 6
- norm_gain: float32 [8192], replicated, may hold values from 0.5 to 1.5
- w_query: float32 [8192, 4096], P(('replica', 'tp')), may hold values from -0.0625 to 0.0625
- w_key: float32 [8192, 512], P(('replica', 'tp')), may hold values from -0.0625 to 0.0625
- w_value: float32 [8192, 512], P(('replica', 'tp')), may hold values from -0.0625 to 0.0625
- bias_query: float32 [4096], P('tp'), may hold values from -3 to 3
- bias_key: float32 [512], P('tp'), may hold values from -3 to 3
- bias_value: float32 [512], P('tp'), may hold values from -3 to 3
- key_pages: bfloat16 [512, 4, 128, 128], P(('replica', 'tp')), may hold values from -256 to 256
- value_pages: bfloat16 [512, 4, 128, 128], P(('replica', 'tp')), may hold values from -6 to 6
- kv_lengths: int32 [96], P(('replica', 'tp')), may hold values from 1 to 1024, as said below
- page_table: int32 [96, 8], P(('replica', 'tp')), may hold values from 0 to 15, as said below
Outputs:
- attended: bfloat16 [96, 4, 4096], P(('replica', 'tp'))
Inputs may be any that keep to these rules, and one draw needn't show every extreme that they name: `kv_lengths`: on every device, one row has exactly 1024 cached tokens. `page_table`: page ids are local to the pool of 16 pages of the device that holds the row. The first ceil(kv_lengths / 128) entries of a row name its pages in order; no page serves two of those entries on one device; later entries are arbitrary pages of the pool.
All inputs are finite; a program needn't handle non-finite values.
Results may differ from a plain program's by a relative error of at most 0.04.
Values may be sent and summed in bfloat16 or wider, within the bound.
No kernel may reach another device: no remote copies, remote signals or barrier semaphores. Data moves between devices by JAX's collectives and lax.ppermute only.
A program may use at most 128 MiB of HBM per device.

v0:
```python
import jax
import jax.numpy as jnp
from jax import lax
from jax.sharding import PartitionSpec as P

HD = 128
HQ = 32
KVH = 4
PAGE = 128
MOSTP = 8
EPS = 1e-06
THETA = 1000000.0


def rotate(values, positions):
    half = values.shape[-1] // 2
    freq = THETA ** (-(jnp.arange(half, dtype=jnp.float32) * 2.0 / values.shape[-1]))
    angle = positions.astype(jnp.float32)[..., None] * freq
    angle = jnp.concatenate([angle, angle], -1)[:, :, None, :]
    turned = jnp.concatenate([-values[..., half:], values[..., :half]], -1)
    return values * jnp.cos(angle) + turned * jnp.sin(angle)


def on_device(
    hidden,
    norm_gain,
    w_query,
    w_key,
    w_value,
    bias_query,
    bias_key,
    bias_value,
    key_pages,
    value_pages,
    kv_lengths,
    page_table,
):
    shards = (
        w_query.astype(jnp.bfloat16),
        w_key.astype(jnp.bfloat16),
        w_value.astype(jnp.bfloat16),
    )
    whole = lax.all_gather(hidden, "tp", axis=2, tiled=True)
    count, steps, width = whole.shape
    wide = whole.astype(jnp.float32)
    power = jnp.mean(wide * wide, axis=2, keepdims=True)
    normed = (
        (wide * lax.rsqrt(power + EPS) * norm_gain)
        .astype(jnp.bfloat16)
        .reshape(count * steps, width)
    )
    local = (
        lax.all_to_all(shards[0], "tp", split_axis=1, concat_axis=0, tiled=True),
        lax.all_to_all(shards[1], "tp", split_axis=1, concat_axis=0, tiled=True),
        lax.all_to_all(shards[2], "tp", split_axis=1, concat_axis=0, tiled=True),
    )
    pieces = (
        lax.all_gather(local[0], "replica", axis=0, tiled=True),
        lax.all_gather(local[1], "replica", axis=0, tiled=True),
        lax.all_gather(local[2], "replica", axis=0, tiled=True),
    )
    sums = tuple((jnp.dot(normed, piece, preferred_element_type=jnp.float32) for piece in pieces))
    made = [
        (total + bias).astype(jnp.bfloat16).reshape(count, steps, -1)
        for total, bias in zip(sums, (bias_query, bias_key, bias_value))
    ]
    query, key_new, value_new = (
        lax.all_to_all(made[0], "tp", split_axis=0, concat_axis=2, tiled=True),
        lax.all_to_all(made[1], "tp", split_axis=0, concat_axis=2, tiled=True),
        lax.all_to_all(made[2], "tp", split_axis=0, concat_axis=2, tiled=True),
    )
    rows = query.shape[0]
    steps = query.shape[1]
    query = query.reshape(rows, steps, HQ, HD)
    key_new = key_new.reshape(rows, steps, KVH, HD)
    value_new = value_new.reshape(rows, steps, KVH, HD)
    positions = kv_lengths[:, None] + jnp.arange(steps, dtype=jnp.int32)[None, :]
    query_rot = rotate(query.astype(jnp.float32), positions).astype(jnp.bfloat16)
    key_rot = rotate(key_new.astype(jnp.float32), positions).astype(jnp.bfloat16)
    group = HQ // KVH
    scale = 1.0 / HD**0.5
    q_heads = query_rot.reshape(rows, steps, KVH, group, HD)
    keys = jnp.take(key_pages, page_table, axis=0)
    vals = jnp.take(value_pages, page_table, axis=0)
    cache = (
        jnp.einsum("rtkgd,rmknd->rtkgmn", q_heads, keys, preferred_element_type=jnp.float32) * scale
    )
    spot = jnp.arange(MOSTP)[:, None] * PAGE + jnp.arange(PAGE)[None, :]
    live = (spot[None] < kv_lengths[:, None, None])[:, None, None, None]
    cache = jnp.where(live, cache, -1e30)
    causal = jnp.arange(steps)[None, :] <= jnp.arange(steps)[:, None]
    fresh = (
        jnp.einsum("rtkgd,rskd->rtkgs", q_heads, key_rot, preferred_element_type=jnp.float32)
        * scale
    )
    fresh = jnp.where(causal[None, :, None, None, :], fresh, -1e30)
    top = jnp.maximum(jnp.max(cache, axis=(4, 5)), jnp.max(fresh, axis=4))
    e_cache = jnp.where(live, jnp.exp(cache - top[..., None, None]), 0.0)
    e_fresh = jnp.where(causal[None, :, None, None, :], jnp.exp(fresh - top[..., None]), 0.0)
    total = jnp.sum(e_cache, axis=(4, 5)) + jnp.sum(e_fresh, axis=4)
    w_cache = (e_cache / total[..., None, None]).astype(jnp.bfloat16)
    w_fresh = (e_fresh / total[..., None]).astype(jnp.bfloat16)
    out = jnp.einsum("rtkgmn,rmknd->rtkgd", w_cache, vals, preferred_element_type=jnp.float32)
    out = out + jnp.einsum(
        "rtkgs,rskd->rtkgd", w_fresh, value_new, preferred_element_type=jnp.float32
    )
    return out.reshape(rows, steps, HQ * HD).astype(jnp.bfloat16)


def solution(mesh):
    in_specs = (
        P("replica", None, "tp"),
        P(),
        P(("replica", "tp"), None),
        P(("replica", "tp"), None),
        P(("replica", "tp"), None),
        P("tp"),
        P("tp"),
        P("tp"),
        P(("replica", "tp"), None, None, None),
        P(("replica", "tp"), None, None, None),
        P(("replica", "tp")),
        P(("replica", "tp"), None),
    )
    out_specs = P(("replica", "tp"), None, None)
    return jax.shard_map(
        on_device, mesh=mesh, in_specs=in_specs, out_specs=out_specs, check_vma=False
    )
```

profile of v0, /device:TPU:0, one launch (start us, length us, event | category | flops | bytes accessed | tf_op | source)
XLA Modules:
  0.0 380.4 jit_solution(5661806267189946849)
XLA Ops:
  6.5 1.3 copy.32
  7.9 10.0 %all_to_all.90 = bf16[256,4,128]{0,2,1:T(8,128)(2,1)S(1)} all-to-all(bf16[256,4,128]{0,2,1:T(8,128)(2,1)S(1)} %bitcast.101), channel_id=1, replica_groups=mesh['replica'=8,'tp'=4] {'tp'}, dimensions={1} | all-to-all | bytes 524288 | tf_op jit(solution)/shard_map/all_to_all | solution.py:54
  17.9 0.8 copy.33
  18.8 0.0 all-gather.8.cloned.1.call-start
  18.8 0.1 copy.37
  19.0 8.4 %all_to_all.91 = bf16[256,4,128]{0,2,1:T(8,128)(2,1)S(1)} all-to-all(bf16[256,4,128]{0,2,1:T(8,128)(2,1)S(1)} %bitcast.102), channel_id=1, replica_groups=mesh['replica'=8,'tp'=4] {'tp'}, dimensions={1} | all-to-all | bytes 524288 | tf_op jit(solution)/shard_map/all_to_all | solution.py:55
  27.4 0.9 copy.38
  28.2 0.0 all-gather.8.cloned.1.call-update
  28.3 0.0 all-gather.4.cloned.1.call-start
  28.3 4.6 %copy.27 = bf16[256,4096]{0,1:T(8,128)(2,1)} copy(f32[256,4096]{1,0:T(8,128)} %param.16) | data formatting | bytes 6291456 | tf_op args[2]
  32.9 30.1 %all_to_all.92 = bf16[256,4,1024]{0,2,1:T(8,128)(2,1)} all-to-all(bf16[256,4,1024]{0,2,1:T(8,128)(2,1)} %bitcast.96), channel_id=1, replica_groups=mesh['replica'=8,'tp'=4] {'tp'}, dimensions={1} | all-to-all | bytes 4194304 | tf_op jit(solution)/shard_map/all_to_all | solution.py:53
  63.1 4.0 %copy.28 = bf16[4,256,1024]{2,1,0:T(8,128)(2,1)} copy(bf16[4,256,1024]{1,2,0:T(8,128)(2,1)} %bitcast.98) | data formatting | bytes 4194304 | tf_op jit(solution)/shard_map/all_to_all | solution.py:53
  67.1 0.9 copy-done.3
  68.0 7.8 %all_gather.12 = bf16[12,4,8192]{2,1,0:T(4,128)(2,1)S(1)} all-gather(bf16[12,4,2048]{2,1,0:T(4,128)(2,1)S(1)} %copy-done.3), channel_id=1, replica_groups=mesh['replica'=8,'tp'=4] {'tp'}, dimensions={2}, use_global_device_ids=true | all-gather | bytes 983040 | tf_op jit(solution)/shard_map/all_gather | solution.py:43
  75.8 0.5 fusion.6
  76.3 1.4 fusion.8
  77.7 1.6 reshape.170
  79.3 0.1 reshape.199
  79.4 2.7 gather_fusion.1
  82.2 4.3 %gather_fusion = bf16[24,4,128,128]{3,2,1,0:T(8,128)(2,1)} fusion(bf16[16,4,128,128]{3,2,1,0:T(8,128)(2,1)} %param.23, s32[1024]{0:T(1024)S(1)} %pad_clamp_fusion), kind=kCustom, calls=%fused_computation.clone | custom fusion | bytes 6291552 | tf_op jit(solution)/shard_map/jit(_take)/gather | solution.py:84
  86.5 0.1 add_convert_fusion
  86.6 0.1 broadcast_multiply_fusion
  86.7 0.1 fusion.47
  86.8 0.1 iota_add_fusion
  86.9 0.1 broadcast_compare_fusion
  87.0 2.7 fusion.24
  89.6 3.4 all-to-all-start.3
  93.0 25.1 %all-gather.8.cloned.1.call-done = bf16[8192,128]{1,0:T(8,128)(2,1)} async-done(((bf16[1024,128]{1,0:T(8,128)(2,1)}), bf16[8192,128]{1,0:T(8,128)(2,1)}) %all-gather.8.cloned.1.call-update) | async-done | bytes 2097168 | tf_op jit(solution)/shard_map/all_gather | solution.py:60
  118.2 2.7 fusion.25
  120.8 225.3 %all-gather.4.cloned.1.call-done = bf16[8192,1024]{1,0:T(8,128)(2,1)} async-done(((bf16[1024,1024]{1,0:T(8,128)(2,1)}), bf16[8192,1024]{1,0:T(8,128)(2,1)}) %all-gather.4.cloned.1.call-update) | async-done | bytes 16777232 | tf_op jit(solution)/shard_map/all_gather | solution.py:58
  346.1 8.8 %fusion.19 = bf16[48,1024]{1,0:T(8,128)(2,1)S(1)} fusion(bf16[48,8192]{1,0:T(8,128)(2,1)S(1)} %reshape.170, bf16[8192,1024]{1,0:T(8,128)(2,1)} %all-gather.4.cloned.1.call-done, f32[1024]{0:T(1024)S(1)} %copy-done.6), kind=kOutput, calls=%fused_computation.27 | convolution fusion | flops 805404672 | bytes 17666048 | tf_op jit(solution)/shard_map/dot_general | solution.py:62
  354.9 0.7 reshape.171
  355.6 3.3 all-to-all-start.1
  358.9 0.1 slice_negate_fusion.1
  359.0 4.2 %all-to-all-done.1 = bf16[12,4,1024]{2,1,0:T(4,128)(2,1)S(1)} async-done(((bf16[12,4,1024]{2,1,0:T(4,128)(2,1)}), bf16[12,4,1024]{2,1,0:T(4,128)(2,1)S(1)}, u32[]{:S(2)}, u32[]{:S(2)}) %all-to-all-start.1) | async-done | bytes 98336 | tf_op jit(solution)/shard_map/all_to_all | solution.py:68
  363.2 3.4 all-to-all-start.5
  366.6 0.1 copy.30
  366.8 0.1 reshape.174
  366.9 0.1 reshape.175
  367.0 0.1 fusion.30
  367.1 0.1 fusion.32
  367.2 0.6 fusion.52
  367.8 3.4 bitcast_reduce_fusion
  371.2 0.2 fusion.35
  371.4 0.4 fusion.15
  371.8 1.0 fusion.16
  372.8 0.3 fusion.21
  373.2 0.7 convert_element_type.107
  (37 shorter events, 0.2 us)
Async XLA Ops:
  6.5 72.9 %copy-start = (bf16[16,4,128,128]{3,2,1,0:T(8,128)(2,1)S(1)}, bf16[16,4,128,128]{3,2,1,0:T(8,128)(2,1)}, u32[]{:S(2)}) copy-start(bf16[16,4,128,128]{3,2,1,0:T(8,128)(2,1)} %param.22) | copy-start | bytes 6291460
  6.5 12.3 %copy-start.2 = (f32[256,512]{1,0:T(8,128)S(1)}, f32[256,512]{1,0:T(8,128)}, u32[]{:S(2)}) copy-start(f32[256,512]{1,0:T(8,128)} %param.18) | copy-start | bytes 1572868
  6.5 80.4 %all-gather.6.cloned.1.call-start = ((), (), s32[]{:S(2)}) async-start(), calls=%async_computation.7 | async-start | bytes 2359296 | tf_op jit(solution)/shard_map/all_gather | solution.py:59
  18.8 99.4 %all-gather.8.cloned.1.call-start = ((), (), s32[]{:S(2)}) async-start(), calls=%async_computation.8 | async-start | bytes 2359296 | tf_op jit(solution)/shard_map/all_gather | solution.py:60
  28.3 317.9 %all-gather.4.cloned.1.call-start = ((), (), s32[]{:S(2)}) async-start(), calls=%async_computation.6 | async-start | bytes 18874368 | tf_op jit(solution)/shard_map/all_gather | solution.py:58
  67.0 0.9 copy-start.3
  67.0 9.3 %copy-start.4 = (f32[8192]{0:T(1024)S(1)}, f32[8192]{0:T(1024)}, u32[]{:S(2)}) copy-start(f32[8192]{0:T(1024)} %param.15) | copy-start | bytes 98308
  75.8 3.5 copy-start.5
  82.2 4.4 %copy-start.7 = (s32[3]{0:T(128)S(1)}, s32[3]{0:T(128)}, u32[]{:S(2)}) copy-start(s32[3]{0:T(128)} %param.24) | copy-start | bytes 40
  82.2 4.8 %copy-start.8 = (f32[128]{0:T(128)S(1)}, f32[128]{0:T(128)}, u32[]{:S(2)}) copy-start(f32[128]{0:T(128)} %param.20) | copy-start | bytes 1540
  86.5 31.7 %copy-start.9 = (f32[128]{0:T(128)S(1)}, f32[128]{0:T(128)}, u32[]{:S(2)}) copy-start(f32[128]{0:T(128)} %param.21) | copy-start | bytes 1540
  89.6 256.5 %copy-start.6 = (f32[1024]{0:T(1024)S(1)}, f32[1024]{0:T(1024)}, u32[]{:S(2)}) copy-start(f32[1024]{0:T(1024)} %param.19) | copy-start | bytes 12292
  89.6 31.2 %all-to-all-start.3 = ((bf16[12,4,128]{2,1,0:T(4,128)(2,1)}), bf16[12,4,128]{2,1,0:T(4,128)(2,1)S(1)}, u32[]{:S(2)}, u32[]{:S(2)}) async-start(bf16[12,4,128]{2,1,0:T(4,128)(2,1)} %bitcast.19), calls=%async_computation.3 | async-start | bytes 24576 | tf_op jit(solution)/shard_map/all_to_all | solution.py:69
  355.6 7.6 %all-to-all-start.1 = ((bf16[12,4,1024]{2,1,0:T(4,128)(2,1)}), bf16[12,4,1024]{2,1,0:T(4,128)(2,1)S(1)}, u32[]{:S(2)}, u32[]{:S(2)}) async-start(bf16[12,4,1024]{2,1,0:T(4,128)(2,1)} %reshape.171), calls=%async_computation.1 | async-start | bytes 196608 | tf_op jit(solution)/shard_map/all_to_all | solution.py:68
  363.2 9.6 %all-to-all-start.5 = ((bf16[12,4,128]{2,1,0:T(4,128)(2,1)}), bf16[12,4,128]{2,1,0:T(4,128)(2,1)S(1)}, u32[]{:S(2)}, u32[]{:S(2)}) async-start(bf16[12,4,128]{2,1,0:T(4,128)(2,1)} %bitcast.30), calls=%async_computation.5 | async-start | bytes 24576 | tf_op jit(solution)/shard_map/all_to_all | solution.py:70
  367.8 4.0 %copy-start.1 = (bf16[24,4,128,128]{3,2,1,0:T(8,128)(2,1)S(1)}, bf16[24,4,128,128]{3,2,1,0:T(8,128)(2,1)}, u32[]{:S(2)}) copy-start(bf16[24,4,128,128]{3,2,1,0:T(8,128)(2,1)} %gather_fusion) | copy-start | bytes 9437188
Sparse Core Ops, SparseCore 0:
  18.9 49.3 all-gather.5
  70.5 47.6 all-gather.7
  120.3 225.7 all-gather.3
where the time goes:
time: 381 us; the launch traced here: 380 us
  waiting for transfers between devices  255 us (67%)
  blocking collectives  56.4 us (15%)
  local copies, waits for them, and re-layouts  23.1 us (6%)
  matrix products  19.4 us (5%)
  between operations  13.4 us (4%)
  starting transfers between devices  10.2 us (3%)
    all_gather x1, waiting for transfers between devices, on_device(): lax.all_gather(local[0], 'replica', axis=0, tiled=True)  225 us
    all_to_all x1, blocking collectives, on_device(): lax.all_to_all(shards[0], 'tp', split_axis=1, concat_axis=0, tiled=True)  30.1 us
    all_gather x1, waiting for transfers between devices, on_device(): lax.all_gather(local[2], 'replica', axis=0, tiled=True)  25.1 us
    dot_general x3, matrix products, on_device(): jnp.dot(normed, piece, preferred_element_type=jnp.float32)  14.1 us
    all_to_all x1, blocking collectives, on_device(): lax.all_to_all(shards[1], 'tp', split_axis=1, concat_axis=0, tiled=True)  10 us
    all_to_all x1, blocking collectives, on_device(): lax.all_to_all(shards[2], 'tp', split_axis=1, concat_axis=0, tiled=True)  8.39 us
    all_gather x1, blocking collectives, on_device(): whole = lax.all_gather(hidden, 'tp', axis=2, tiled=True)  7.81 us
  transfers between devices with their start and end apart: 6, of which 3 were waited for; matrix products, arithmetic and copies ran while one was open for 8% of the time, Pallas kernels for 0%

commit v1 on v0

--- a/solution.py
+++ b/solution.py
@@ -10,6 +10,19 @@
 MOSTP = 8
 EPS = 1e-06
 THETA = 1000000.0
+
+
+def collect(shard, axis, dim):
+    ways = lax.axis_size(axis)
+    up = [(d, (d + 1) % ways) for d in range(ways)]
+    down = [(d, (d - 1) % ways) for d in range(ways)]
+    earlier, later = ([shard], [shard])
+    for _ in range(ways // 2):
+        earlier.append(lax.ppermute(earlier[-1], axis, up))
+    for _ in range((ways - 1) // 2):
+        later.append(lax.ppermute(later[-1], axis, down))
+    line = jnp.concatenate([*earlier[::-1], *later[1:]], axis=dim)
+    return jnp.roll(line, (lax.axis_index(axis) - ways // 2) * shard.shape[dim], axis=dim)
 
 
 def rotate(values, positions):
@@ -55,7 +68,7 @@
         lax.all_to_all(shards[2], "tp", split_axis=1, concat_axis=0, tiled=True),
     )
     pieces = (
-        lax.all_gather(local[0], "replica", axis=0, tiled=True),
+        collect(local[0], "replica", 0),
         lax.all_gather(local[1], "replica", axis=0, tiled=True),
         lax.all_gather(local[2], "replica", axis=0, tiled=True),
     )

time: 381 us -> 484 us (1.27)
  local copies, waits for them, and re-layouts: 23.1 us -> 68.5 us
  waiting for transfers between devices: 255 us -> 289 us
  starting transfers between devices: 10.2 us -> 41.4 us
  blocking collectives: 56.4 us -> 47.7 us
    ppermute x0 -> x7, waiting for transfers between devices: none -> 249 us  [the longest x4 247 us: collect(): earlier.append(lax.ppermute(earlier[-1], axis, up))]
    all_gather x1 -> x0, waiting for transfers between devices: 225 us -> none  [on_device(): lax.all_gather(local[0], 'replica', axis=0, tiled=True)]
    unnamed x23 -> x42, local copies, waits for them, and re-layouts: 7.03 us -> 49.3 us
    ppermute x0 -> x7, starting transfers between devices: none -> 28 us  [the longest x3 20.7 us: collect(): later.append(lax.ppermute(later[-1], axis, down))]
    all_gather x1, waiting for transfers between devices: 25.1 us -> 35.5 us  [on_device(): lax.all_gather(local[2], 'replica', axis=0, tiled=True)]
    all_to_all x1 -> x0, blocking collectives: 8.39 us -> none  [on_device(): lax.all_to_all(shards[2], 'tp', split_axis=1, concat_axis=0, tiled=True)]
  transfers between devices with their start and end apart: 6 -> 13, of which waited for: 3 -> 7; matrix products, arithmetic and copies ran while one was open for 8% -> 9% of each run, Pallas kernels for 0% -> 0%
where the time goes in v1:
time: 484 us; the launch traced here: 483 us
  waiting for transfers between devices  289 us (60%)
  local copies, waits for them, and re-layouts  68.5 us (14%)
  blocking collectives  47.7 us (10%)
  starting transfers between devices  41.4 us (9%)
  matrix products  19.3 us (4%)
  between operations  13.7 us (3%)
    ppermute x4, waiting for transfers between devices, collect(): earlier.append(lax.ppermute(earlier[-1], axis, up))  247 us
    unnamed x42, local copies, waits for them, and re-layouts  49.3 us
    all_gather x1, waiting for transfers between devices, on_device(): lax.all_gather(local[2], 'replica', axis=0, tiled=True)  35.5 us
    all_to_all x1, blocking collectives, on_device(): lax.all_to_all(shards[0], 'tp', split_axis=1, concat_axis=0, tiled=True)  30.8 us
    ppermute x3, starting transfers between devices, collect(): later.append(lax.ppermute(later[-1], axis, down))  20.7 us
    dot_general x3, matrix products, on_device(): jnp.dot(normed, piece, preferred_element_type=jnp.float32)  14.1 us
  transfers between devices with their start and end apart: 13, of which 7 were waited for; matrix products, arithmetic and copies ran while one was open for 9% of the time, Pallas kernels for 0%

profile of v1, /device:TPU:0, one launch (start us, length us, event | category | flops | bytes accessed | tf_op | source)
XLA Modules:
  0.0 482.8 jit_solution(1587899412225080560)
XLA Ops:
  6.5 4.8 copy.27
  11.3 30.8 %all_to_all.90 = bf16[256,4,1024]{0,2,1:T(8,128)(2,1)} all-to-all(bf16[256,4,1024]{0,2,1:T(8,128)(2,1)} %bitcast.99), channel_id=1, replica_groups=mesh['replica'=8,'tp'=4] {'tp'}, dimensions={1} | all-to-all | bytes 4194304 | tf_op jit(solution)/shard_map/all_to_all | solution.py:66
  42.1 4.1 copy.28
  46.2 2.3 collective-permute-start
  48.7 8.4 %all_to_all.91 = bf16[256,4,128]{0,2,1:T(8,128)(2,1)S(1)} all-to-all(bf16[256,4,128]{0,2,1:T(8,128)(2,1)S(1)} %bitcast.103), channel_id=1, replica_groups=mesh['replica'=8,'tp'=4] {'tp'}, dimensions={1} | all-to-all | bytes 524288 | tf_op jit(solution)/shard_map/all_to_all | solution.py:67
  57.9 47.7 %collective-permute-done = bf16[1024,1024]{1,0:T(8,128)(2,1)} collective-permute-done((bf16[1024,1024]{1,0:T(8,128)(2,1)}, bf16[1024,1024]{1,0:T(8,128)(2,1)}, u32[]{:S(2)}, u32[]{:S(2)}) %collective-permute-start) | collective-permute-done | bytes 2097184 | tf_op jit(solution)/shard_map/ppermute | solution.py:21
  105.6 4.7 collective-permute-start.4
  110.3 0.8 copy.37
  111.1 3.4 all-to-all-start.4
  114.6 91.7 %collective-permute-done.1 = bf16[1024,1024]{1,0:T(8,128)(2,1)} collective-permute-done((bf16[1024,1024]{1,0:T(8,128)(2,1)}, bf16[1024,1024]{1,0:T(8,128)(2,1)}, u32[]{:S(2)}, u32[]{:S(2)}) %collective-permute-start.1) | collective-permute-done | bytes 2097184 | tf_op jit(solution)/shard_map/ppermute | solution.py:21
  206.3 2.5 collective-permute-start.2
  208.8 8.5 %all_gather.9 = bf16[12,4,8192]{2,1,0:T(4,128)(2,1)S(1)} all-gather(bf16[12,4,2048]{2,1,0:T(4,128)(2,1)} %param.14), channel_id=1, replica_groups=mesh['replica'=8,'tp'=4] {'tp'}, dimensions={2}, use_global_device_ids=true | all-gather | bytes 983040 | tf_op jit(solution)/shard_map/all_gather | solution.py:56
  219.1 14.4 %collective-permute-start.5 = (bf16[1024,1024]{1,0:T(8,128)(2,1)}, bf16[1024,1024]{1,0:T(8,128)(2,1)}, u32[]{:S(2)}, u32[]{:S(2)}) collective-permute-start(bf16[1024,1024]{1,0:T(8,128)(2,1)} %collective-permute-done.4), channel_id=1, source_target_pairs={{0,28},{4,0},{8,4},{12,8},{16,12},{20,16},{24,20},{28,24},{1,29},{... | collective-permute-start | bytes 6291464 | tf_op jit(solution)/shard_map/ppermute | solution.py:23
  233.5 79.6 %collective-permute-done.2 = bf16[1024,1024]{1,0:T(8,128)(2,1)} collective-permute-done((bf16[1024,1024]{1,0:T(8,128)(2,1)}, bf16[1024,1024]{1,0:T(8,128)(2,1)}, u32[]{:S(2)}, u32[]{:S(2)}) %collective-permute-start.2) | collective-permute-done | bytes 2097184 | tf_op jit(solution)/shard_map/ppermute | solution.py:21
  313.1 2.5 collective-permute-start.3
  315.6 1.4 fusion.10
  317.0 2.1 collective-permute-done.5
  319.0 1.6 collective-permute-start.6
  320.6 1.6 reshape.170
  322.2 2.7 gather_fusion.1
  324.9 4.3 gather_fusion
  329.4 2.7 fusion.31
  332.1 3.4 all-to-all-start.3
  335.5 35.5 %all-gather.5.cloned.1.call-done = bf16[8192,128]{1,0:T(8,128)(2,1)} async-done(((bf16[1024,128]{1,0:T(8,128)(2,1)}), bf16[8192,128]{1,0:T(8,128)(2,1)}) %all-gather.5.cloned.1.call-update) | async-done | bytes 2097168 | tf_op jit(solution)/shard_map/all_gather | solution.py:73
  371.0 2.7 fusion.32
  373.7 28.2 %collective-permute-done.3 = bf16[1024,1024]{1,0:T(8,128)(2,1)} collective-permute-done((bf16[1024,1024]{1,0:T(8,128)(2,1)}, bf16[1024,1024]{1,0:T(8,128)(2,1)}, u32[]{:S(2)}, u32[]{:S(2)}) %collective-permute-start.3) | collective-permute-done | bytes 2097184 | tf_op jit(solution)/shard_map/ppermute | solution.py:21
  401.9 3.1 constant_dynamic-update-slice_fusion.15
  405.0 3.1 constant_dynamic-update-slice_fusion.14
  408.0 3.2 constant_dynamic-update-slice_fusion.13
  411.3 3.1 constant_dynamic-update-slice_fusion.12
  414.4 1.6 constant_dynamic-update-slice_fusion.11
  416.0 3.1 constant_dynamic-update-slice_fusion.10
  419.1 3.1 constant_dynamic-update-slice_fusion.9
  422.2 3.1 constant_dynamic-update-slice_fusion.8
  425.2 3.1 constant_dynamic-update-slice_fusion.7
  428.3 3.1 constant_dynamic-update-slice_fusion.6
  431.4 3.1 constant_dynamic-update-slice_fusion.5
  434.5 3.1 constant_dynamic-update-slice_fusion.4
  437.6 1.6 constant_dynamic-update-slice_fusion.3
  439.2 3.1 constant_dynamic-update-slice_fusion.2
  442.3 3.1 constant_dynamic-update-slice_fusion.1
  445.4 3.1 constant_dynamic-update-slice_fusion
  448.5 8.8 %fusion.24 = bf16[48,1024]{1,0:T(8,128)(2,1)S(1)} fusion(bf16[48,8192]{1,0:T(8,128)(2,1)S(1)} %reshape.170, bf16[16384,1024]{1,0:T(8,128)(2,1)} %constant_dynamic-update-slice_fusion, s32[]{:T(128)S(6)} %select_n.38, f32[1024]{0:T(1024)S(1)} %copy-done.11), kind=kOutput, calls=%fused_computation.29 | convolution fusion | flops 805404672 | bytes 17666052 | tf_op jit(solution)/shard_map/dot_general | solution.py:75
  457.9 3.3 all-to-all-start.1
  461.3 4.2 all-to-all-done.1
  465.5 3.2 all-to-all-start.5
  470.0 3.4 bitcast_reduce_fusion
  474.0 1.0 fusion.18
  (69 shorter events, 6.5 us)
Async XLA Ops:
  6.5 315.7 %copy-start = (bf16[16,4,128,128]{3,2,1,0:T(8,128)(2,1)S(1)}, bf16[16,4,128,128]{3,2,1,0:T(8,128)(2,1)}, u32[]{:S(2)}) copy-start(bf16[16,4,128,128]{3,2,1,0:T(8,128)(2,1)} %param.22) | copy-start | bytes 6291460
  6.5 322.9 %all-gather.3.cloned.1.call-start = ((), (), s32[]{:S(2)}) async-start(), calls=%async_computation.6 | async-start | bytes 2359296 | tf_op jit(solution)/shard_map/all_gather | solution.py:72
  42.1 6.4 %copy-start.4 = (f32[256,512]{1,0:T(8,128)S(1)}, f32[256,512]{1,0:T(8,128)}, u32[]{:S(2)}) copy-start(f32[256,512]{1,0:T(8,128)} %param.17) | copy-start | bytes 1572868
  42.1 68.2 %copy-start.5 = (f32[256,512]{1,0:T(8,128)S(1)}, f32[256,512]{1,0:T(8,128)}, u32[]{:S(2)}) copy-start(f32[256,512]{1,0:T(8,128)} %param.18) | copy-start | bytes 1572868
  42.1 72.5 %copy-start.7 = (s32[3,8]{1,0:T(4,128)S(1)}, s32[3,8]{1,0:T(4,128)}, u32[]{:S(2)}) copy-start(s32[3,8]{1,0:T(4,128)} %param.25) | copy-start | bytes 292
  46.2 172.6 %copy-start.8 = (s32[3]{0:T(128)S(1)}, s32[3]{0:T(128)}, u32[]{:S(2)}) copy-start(s32[3]{0:T(128)} %param.24) | copy-start | bytes 40
  46.2 269.4 %copy-start.6 = (f32[8192]{0:T(1024)S(1)}, f32[8192]{0:T(1024)}, u32[]{:S(2)}) copy-start(f32[8192]{0:T(1024)} %param.15) | copy-start | bytes 98308
  46.2 59.4 %collective-permute-start = (bf16[1024,1024]{1,0:T(8,128)(2,1)}, bf16[1024,1024]{1,0:T(8,128)(2,1)}, u32[]{:S(2)}, u32[]{:S(2)}) collective-permute-start(bf16[1024,1024]{1,0:T(8,128)(2,1)} %bitcast.95), channel_id=1, source_target_pairs={{0,4},{4,8},{8,12},{12,16},{16,20},{20,24},{24,28},{28,0},{1,5},{5... | collective-permute-start | bytes 6291464 | tf_op jit(solution)/shard_map/ppermute | solution.py:21
  105.6 100.7 %collective-permute-start.1 = (bf16[1024,1024]{1,0:T(8,128)(2,1)}, bf16[1024,1024]{1,0:T(8,128)(2,1)}, u32[]{:S(2)}, u32[]{:S(2)}) collective-permute-start(bf16[1024,1024]{1,0:T(8,128)(2,1)} %collective-permute-done), channel_id=1, source_target_pairs={{0,4},{4,8},{8,12},{12,16},{16,20},{20,24},{24,28},{28,0},{1,5},{5... | collective-permute-start | bytes 6291464 | tf_op jit(solution)/shard_map/ppermute | solution.py:21
  105.6 113.5 %collective-permute-start.4 = (bf16[1024,1024]{1,0:T(8,128)(2,1)}, bf16[1024,1024]{1,0:T(8,128)(2,1)}, u32[]{:S(2)}, u32[]{:S(2)}) collective-permute-start(bf16[1024,1024]{1,0:T(8,128)(2,1)} %bitcast.96), channel_id=1, source_target_pairs={{0,28},{4,0},{8,4},{12,8},{16,12},{20,16},{24,20},{28,24},{1,29},{... | collective-permute-start | bytes 6291464 | tf_op jit(solution)/shard_map/ppermute | solution.py:23
  111.1 106.8 %all-to-all-start.4 = ((bf16[256,4,128]{0,2,1:T(8,128)(2,1)}), bf16[256,4,128]{0,2,1:T(8,128)(2,1)S(1)}, u32[]{:S(2)}, u32[]{:S(2)}) async-start(bf16[256,4,128]{0,2,1:T(8,128)(2,1)} %bitcast.27), calls=%async_computation.4 | async-start | bytes 524288 | tf_op jit(solution)/shard_map/all_to_all | solution.py:68
  114.6 256.5 %all-gather.5.cloned.1.call-start = ((), (), s32[]{:S(2)}) async-start(), calls=%async_computation.7 | async-start | bytes 2359296 | tf_op jit(solution)/shard_map/all_gather | solution.py:73
  206.3 106.8 %collective-permute-start.2 = (bf16[1024,1024]{1,0:T(8,128)(2,1)}, bf16[1024,1024]{1,0:T(8,128)(2,1)}, u32[]{:S(2)}, u32[]{:S(2)}) collective-permute-start(bf16[1024,1024]{1,0:T(8,128)(2,1)} %collective-permute-done.1), channel_id=1, source_target_pairs={{0,4},{4,8},{8,12},{12,16},{16,20},{20,24},{24,28},{28,0},{1,5},{5... | collective-permute-start | bytes 6291464 | tf_op jit(solution)/shard_map/ppermute | solution.py:21
  219.1 99.9 %collective-permute-start.5 = (bf16[1024,1024]{1,0:T(8,128)(2,1)}, bf16[1024,1024]{1,0:T(8,128)(2,1)}, u32[]{:S(2)}, u32[]{:S(2)}) collective-permute-start(bf16[1024,1024]{1,0:T(8,128)(2,1)} %collective-permute-done.4), channel_id=1, source_target_pairs={{0,28},{4,0},{8,4},{12,8},{16,12},{20,16},{24,20},{28,24},{1,29},{... | collective-permute-start | bytes 6291464 | tf_op jit(solution)/shard_map/ppermute | solution.py:23
  313.1 88.8 %collective-permute-start.3 = (bf16[1024,1024]{1,0:T(8,128)(2,1)}, bf16[1024,1024]{1,0:T(8,128)(2,1)}, u32[]{:S(2)}, u32[]{:S(2)}) collective-permute-start(bf16[1024,1024]{1,0:T(8,128)(2,1)} %collective-permute-done.2), channel_id=1, source_target_pairs={{0,4},{4,8},{8,12},{12,16},{16,20},{20,24},{24,28},{28,0},{1,5},{5... | collective-permute-start | bytes 6291464 | tf_op jit(solution)/shard_map/ppermute | solution.py:21
  319.0 103.1 %collective-permute-start.6 = (bf16[1024,1024]{1,0:T(8,128)(2,1)}, bf16[1024,1024]{1,0:T(8,128)(2,1)}, u32[]{:S(2)}, u32[]{:S(2)}) collective-permute-start(bf16[1024,1024]{1,0:T(8,128)(2,1)} %collective-permute-done.5), channel_id=1, source_target_pairs={{0,28},{4,0},{8,4},{12,8},{16,12},{20,16},{24,20},{28,24},{1,29},{... | collective-permute-start | bytes 6291464 | tf_op jit(solution)/shard_map/ppermute | solution.py:23
  324.9 4.5 copy-start.9
  324.9 46.1 %copy-start.10 = (f32[128]{0:T(128)S(1)}, f32[128]{0:T(128)}, u32[]{:S(2)}) copy-start(f32[128]{0:T(128)} %param.21) | copy-start | bytes 1540
  332.1 41.6 %all-to-all-start.3 = ((bf16[12,4,128]{2,1,0:T(4,128)(2,1)}), bf16[12,4,128]{2,1,0:T(4,128)(2,1)S(1)}, u32[]{:S(2)}, u32[]{:S(2)}) async-start(bf16[12,4,128]{2,1,0:T(4,128)(2,1)} %bitcast.19), calls=%async_computation.3 | async-start | bytes 24576 | tf_op jit(solution)/shard_map/all_to_all | solution.py:82
  408.0 6.4 %copy-start.2 = (bf16[4,256,1024]{2,1,0:T(8,128)(2,1)S(1)}, bf16[4,256,1024]{2,1,0:T(8,128)(2,1)}, u32[]{:S(2)}) copy-start(bf16[4,256,1024]{2,1,0:T(8,128)(2,1)} %copy.28) | copy-start | bytes 6291460
  445.4 3.1 copy-start.11
  457.9 7.6 %all-to-all-start.1 = ((bf16[12,4,1024]{2,1,0:T(4,128)(2,1)}), bf16[12,4,1024]{2,1,0:T(4,128)(2,1)S(1)}, u32[]{:S(2)}, u32[]{:S(2)}) async-start(bf16[12,4,1024]{2,1,0:T(4,128)(2,1)} %reshape.171), calls=%async_computation.1 | async-start | bytes 196608 | tf_op jit(solution)/shard_map/all_to_all | solution.py:81
  465.5 9.5 %all-to-all-start.5 = ((bf16[12,4,128]{2,1,0:T(4,128)(2,1)}), bf16[12,4,128]{2,1,0:T(4,128)(2,1)S(1)}, u32[]{:S(2)}, u32[]{:S(2)}) async-start(bf16[12,4,128]{2,1,0:T(4,128)(2,1)} %bitcast.30), calls=%async_computation.5 | async-start | bytes 24576 | tf_op jit(solution)/shard_map/all_to_all | solution.py:83
  470.0 4.0 copy-start.3
  474.0 2.0 copy-start.1
Sparse Core Ops, SparseCore 0:
  58.0 125.7 all-gather.2
  218.9 152.0 all-gather.4
